TPU v7x, 32 devices: a whole 2x2x4 slice. The times are simulated.
32 devices in a mesh: tm: 16 (over z, y, x), row: 2 (over core).
Axes of the slice: x: 2, y: 2, z: 4, core: 2. Of those that a mesh axis runs over, the one named last changes fastest.
Arguments:
- initial: float32 [1024], replicated, may hold values from -6 to 6
- dynamics: float32 [1024, 1024], replicated, may hold values from -0.009765625 to 0.009765625
- obs_rows: bfloat16 [32768, 1024], P('tm', 'row'), may hold values from -0.1875 to 0.1875
- obs_values: bfloat16 [32768], P('tm'), may hold values from -6 to 6
- obs_slab: int32 [32768, 1], P('tm'), may hold values from 0 to 31; in each aligned block of 2048 rows (0 to 2047, 2048 to 4095, ...) at most 64 rows name the same one
Outputs:
- states: float32 [32, 1024], P('tm', 'row')
Inputs may be any that keep to these rules, and one draw needn't show every extreme that they name: `obs_slab`: within the rows ingested by one index of tm, no slab is named by more than 64 rows, a bound that some block reaches of them.
All inputs are finite; a program needn't handle non-finite values.
Results may differ from a plain program's by a relative error of at most 0.0003.
Values may be sent and summed in bfloat16 or wider, within the bound.
A program may use at most 128 MiB of HBM per device.

v0:
```python
import jax
import jax.numpy as jnp
from jax import lax
from jax.sharding import PartitionSpec as P

SLAB_DEV = 2
CAP = 64
sigma_gain = 0.3


def shifted(value, axis, steps):
    count = lax.axis_size(axis)
    first, last = (max(0, -steps), min(count, count - steps))
    return lax.ppermute(value, axis, [(source, source + steps) for source in range(first, last)])


def left_product(left_rows, pieces):
    new_matrix = jnp.dot(left_rows, pieces[0], precision=lax.Precision.HIGHEST)
    new_vector = jnp.dot(left_rows, pieces[1], precision=lax.Precision.HIGHEST)
    return (new_matrix, new_vector)


def body(initial, dynamics, obs_rows, obs_values, obs_slab):
    time_devs = lax.axis_size("tm")
    row_devs = lax.axis_size("row")
    state_width = dynamics.shape[1]
    local_cols = state_width // row_devs
    row_start = lax.axis_index("row") * local_cols
    time_index = lax.axis_index("tm")
    capacity = CAP
    slab_total = SLAB_DEV * time_devs
    obs_count = obs_rows.shape[0]
    target = obs_slab[:, 0]
    onehot = (target[:, None] == jnp.arange(slab_total, dtype=jnp.int32)[None, :]).astype(jnp.int32)
    rank_in = jnp.sum(onehot * (jnp.cumsum(onehot, axis=0) - 1), axis=1)
    owner_dev = target // SLAB_DEV
    within = target % SLAB_DEV
    slot_index = (within * time_devs + owner_dev) * capacity + rank_in
    slot_table = (
        jnp.full((slab_total * capacity,), obs_count, jnp.int32)
        .at[slot_index]
        .set(jnp.arange(obs_count, dtype=jnp.int32))
    )
    padded_rows = jnp.concatenate([obs_rows, jnp.zeros((1, local_cols), jnp.bfloat16)], axis=0)
    padded_values = jnp.concatenate([obs_values, jnp.zeros((1,), jnp.bfloat16)], axis=0)
    send_rows = padded_rows[slot_table].reshape(SLAB_DEV, time_devs, capacity, local_cols)
    send_values = padded_values[slot_table].reshape(SLAB_DEV, time_devs, capacity)
    recv_rows, recv_values = (
        lax.all_to_all(send_rows, "tm", split_axis=1, concat_axis=1, tiled=True),
        lax.all_to_all(send_values, "tm", split_axis=1, concat_axis=1, tiled=True),
    )
    slab_rows = recv_rows.reshape(SLAB_DEV, time_devs * capacity, local_cols)
    slab_values = recv_values.reshape(SLAB_DEV, time_devs * capacity)
    information = jnp.einsum(
        "sra,srb->sab",
        slab_rows,
        lax.all_gather(slab_rows, "row", axis=2, tiled=True),
        preferred_element_type=jnp.float32,
    )
    moment = jnp.einsum("sr,sra->sa", slab_values, slab_rows, preferred_element_type=jnp.float32)
    evolve = jnp.eye(state_width, dtype=jnp.float32) + dynamics
    evolve_rows = lax.dynamic_slice_in_dim(evolve, row_start, local_cols, 0)
    transitions = []
    offsets = []
    for slab_index in range(SLAB_DEV):
        transitions.append(
            evolve_rows
            - sigma_gain * jnp.dot(information[slab_index], evolve, precision=lax.Precision.HIGHEST)
        )
        offsets.append(sigma_gain * moment[slab_index])
    composed = transitions[0]
    composed_offset = offsets[0]
    slab_index = 1
    new_matrix, new_vector = left_product(
        transitions[slab_index],
        (
            lax.all_gather(composed, "row", axis=0, tiled=True),
            lax.all_gather(composed_offset, "row", axis=0, tiled=True),
        ),
    )
    composed = new_matrix
    composed_offset = new_vector + offsets[slab_index]
    initial_rows = lax.dynamic_slice_in_dim(initial, row_start, local_cols, 0)

    def advance(turn, state_rows):
        whole_state = lax.all_gather(state_rows, "row", axis=0, tiled=True)
        leaving = jnp.dot(composed, whole_state, precision=lax.Precision.HIGHEST) + composed_offset
        arriving = shifted(leaving, "tm", 1)
        return jnp.where(time_index == 0, initial_rows, arriving)

    entry_rows = lax.fori_loop(0, time_devs - 1, advance, initial_rows)
    states = []
    current = entry_rows
    for slab_index in range(SLAB_DEV):
        whole_state = lax.all_gather(current, "row", axis=0, tiled=True)
        current = (
            jnp.dot(transitions[slab_index], whole_state, precision=lax.Precision.HIGHEST)
            + offsets[slab_index]
        )
        states.append(current)
    return jnp.stack(states)


def solution(mesh):
    placed = (P(), P(), P("tm", "row"), P("tm"), P("tm", None))
    return jax.shard_map(
        body, mesh=mesh, in_specs=placed, out_specs=P("tm", "row"), check_vma=False
    )
```

profile of v0, /device:TPU:9, one launch (start us, length us, event | category | flops | bytes accessed | tf_op | source)
XLA Modules:
  0.0 357.0 jit_solution(5598932367776925572)
XLA Ops:
  7.3 9.1 %reduce-window.6 = s32[32,16,128]{2,1,0:T(8,128)S(1)} reduce-window(s32[32,16,128]{2,1,0:T(8,128)S(1)} %fusion.4, s32[]{:T(128)} %copy.37), window={size=1x1x128 pad=0_0x0_0x127_0}, to_apply=%region_0.0 | reduce-window | flops 8323072 | bytes 524292 | tf_op jit(solution)/shard_map/reduce-window
  17.3 8.0 %scatter_custom_fusion = s32[2048]{0:T(1024)S(1)} fusion(s32[2048]{0:T(1024)S(1)} %bitcast.110, s32[2048]{0:T(1024)S(1)} %iota.23, s32[]{:T(128)} %constant.63.clone.1), kind=kCustom, calls=%fused_computation.34 | custom fusion | bytes 8196 | tf_op jit(solution)/shard_map/scatter | solution.py:42
  27.1 9.2 %gather_fusion = bf16[2048,512]{1,0:T(8,128)(2,1)} fusion(bf16[2049,512]{1,0:T(8,128)(2,1)S(1)} %concatenate.6, s32[2048]{0:T(1024)S(1)} %fusion.5), kind=kCustom, calls=%fused_computation | custom fusion | bytes 4202496 | tf_op jit(solution)/shard_map/gather | solution.py:46
  38.2 53.8 %all_to_all.10 = bf16[2,16,64,512]{3,2,0,1:T(8,128)(2,1)S(1)} all-to-all(bf16[2,16,64,512]{3,2,0,1:T(8,128)(2,1)S(1)} %copy.17), channel_id=1, replica_groups=mesh['tm'=16,'row'=2] {'tm'}, dimensions={1} | all-to-all | bytes 4194304 | tf_op jit(solution)/shard_map/all_to_all | solution.py:49
  93.7 5.0 %convert_add_fusion = f32[1024,1024]{1,0:T(8,128)} fusion(f32[1024,1024]{1,0:T(8,128)} %param.8), kind=kLoop, calls=%fused_computation.4 | loop fusion | flops 3145728 | bytes 8388608 | tf_op jit(solution)/shard_map/add | solution.py:61
  98.6 9.4 %all-gather.9.cloned.1.call-done = bf16[2,1024,1024]{2,1,0:T(8,128)(2,1)} async-done(((bf16[2,1024,512]{2,1,0:T(8,128)(2,1)}), bf16[2,1024,1024]{2,1,0:T(8,128)(2,1)}) %all-gather.9.cloned.1.call-update) | async-done | bytes 4194320 | tf_op jit(solution)/shard_map/all_gather | solution.py:57
  108.0 4.7 %fusion.13 = f32[2,512,1024]{2,1,0:T(8,128)S(1)} fusion(bf16[2,1024,512]{2,1,0:T(8,128)(2,1)S(1)} %bitcast.86, bf16[2,1024,1024]{2,1,0:T(8,128)(2,1)} %all-gather.9.cloned.1.call-done), kind=kOutput, calls=%fused_computation.39 | convolution fusion | flops 2147483648 | bytes 10485760 | tf_op jit(solution)/shard_map/sra,srb->sab/dot_general | solution.py:54
  112.8 1.9 copy-done.4
  114.7 8.2 %multiply_subtract_fusion.1 = f32[512,1024]{1,0:T(8,128)} fusion(f32[1024,1024]{1,0:T(8,128)S(1)} %copy-done, s32[]{:T(128)S(6)} %select_n.38, f32[2,512,1024]{2,1,0:T(8,128)S(1)} %fusion.13), kind=kOutput, calls=%fused_computation.11 | convolution fusion | flops 6443499520 | bytes 10485764 | tf_op jit(solution)/shard_map/dot_general | solution.py:68
  123.6 13.1 %gather_fusion.1 = bf16[2048]{0:T(1024)(128)(2,1)S(1)} fusion(bf16[2049]{0:T(1024)(128)(2,1)S(1)} %pad_maximum_fusion, s32[2048]{0:T(1024)S(1)} %fusion.5), kind=kCustom, calls=%fused_computation.1 | custom fusion | bytes 16384 | tf_op jit(solution)/shard_map/gather | solution.py:47
  137.4 6.4 %all-to-all-start.1 = ((bf16[2,16,64]{2,0,1:T(2,128)(2,1)}), bf16[2,16,64]{2,0,1:T(2,128)(2,1)S(1)}, u32[]{:S(2)}, u32[]{:S(2)}) async-start(bf16[2,16,64]{2,0,1:T(2,128)(2,1)} %copy.20), calls=%async_computation.1 | async-start | bytes 16384 | tf_op jit(solution)/shard_map/all_to_all | solution.py:50
  143.9 5.0 %all-to-all-done.1 = bf16[2,16,64]{2,0,1:T(2,128)(2,1)S(1)} async-done(((bf16[2,16,64]{2,0,1:T(2,128)(2,1)}), bf16[2,16,64]{2,0,1:T(2,128)(2,1)S(1)}, u32[]{:S(2)}, u32[]{:S(2)}) %all-to-all-start.1) | async-done | bytes 4128 | tf_op jit(solution)/shard_map/all_to_all | solution.py:50
  149.4 3.1 all-gather
  152.5 10.1 %multiply_subtract_fusion = f32[512,1024]{1,0:T(8,128)S(1)} fusion(f32[1024,1024]{1,0:T(8,128)} %convert_add_fusion, s32[]{:T(128)S(6)} %select_n.38, f32[2,512,1024]{2,1,0:T(8,128)} %copy-done.4), kind=kOutput, calls=%fused_computation.10 | convolution fusion | flops 6443499520 | bytes 10485764 | tf_op jit(solution)/shard_map/dot_general | solution.py:68
  164.0 1.9 fusion.8
  165.9 9.7 %fusion.14 = f32[512,1024]{1,0:T(8,128)S(1)} fusion(f32[512,1024]{1,0:T(8,128)} %copy-done.1, f32[1024,1024]{1,0:T(8,128)} %all-gather.11.cloned.1.call-done), kind=kOutput, calls=%fused_computation.40 | convolution fusion | flops 6442450944 | bytes 8388608 | tf_op jit(solution)/shard_map/dot_general | solution.py:18
  175.6 163.7 %while.12 = (s32[]{:T(128)}, f32[512]{0:T(512)S(1)}, pred[]{:T(512)}, f32[512,1024]{1,0:T(8,128)S(1)}, f32[512]{0:T(512)S(1)}, /*index=5*/f32[512]{0:T(512)S(1)}, s32[]{:T(128)}) while((s32[]{:T(128)}, f32[512]{0:T(512)S(1)}, pred[]{:T(512)}, f32[512,1024]{1,0:T(8,128)S(1)}, f32[512]{0:T(512)S(1)}, /*index=5*/f32[512]{0:T(512)S(1)}, ...), condition=%wide.region_5.6_spmd, body=%wide.region_4.5_spmd.sunk | while | flops 6292482 | bytes 2130038 | solution.py:91
  179.3 2.2 collective-permute-start
  181.5 3.9 %collective-permute-done = f32[512]{0:T(512)S(1)} collective-permute-done((f32[512]{0:T(512)S(1)}, f32[512]{0:T(512)S(1)}, u32[]{:S(2)}, u32[]{:S(2)}) %collective-permute-start) | collective-permute-done | bytes 2080 | tf_op jit(solution)/shard_map/while/body/eval_jaxpr/ppermute | solution.py:14
  185.4 3.0 all-gather.5
  190.3 1.9 collective-permute-start
  192.2 4.2 %collective-permute-done = f32[512]{0:T(512)S(1)} collective-permute-done((f32[512]{0:T(512)S(1)}, f32[512]{0:T(512)S(1)}, u32[]{:S(2)}, u32[]{:S(2)}) %collective-permute-start) | collective-permute-done | bytes 2080 | tf_op jit(solution)/shard_map/while/body/eval_jaxpr/ppermute | solution.py:14
  196.4 3.0 all-gather.5
  201.3 1.9 collective-permute-start
  203.2 4.2 %collective-permute-done = f32[512]{0:T(512)S(1)} collective-permute-done((f32[512]{0:T(512)S(1)}, f32[512]{0:T(512)S(1)}, u32[]{:S(2)}, u32[]{:S(2)}) %collective-permute-start) | collective-permute-done | bytes 2080 | tf_op jit(solution)/shard_map/while/body/eval_jaxpr/ppermute | solution.py:14
  207.4 3.0 all-gather.5
  212.2 1.9 collective-permute-start
  214.2 4.2 %collective-permute-done = f32[512]{0:T(512)S(1)} collective-permute-done((f32[512]{0:T(512)S(1)}, f32[512]{0:T(512)S(1)}, u32[]{:S(2)}, u32[]{:S(2)}) %collective-permute-start) | collective-permute-done | bytes 2080 | tf_op jit(solution)/shard_map/while/body/eval_jaxpr/ppermute | solution.py:14
  218.4 3.0 all-gather.5
  223.2 1.9 collective-permute-start
  225.2 4.2 %collective-permute-done = f32[512]{0:T(512)S(1)} collective-permute-done((f32[512]{0:T(512)S(1)}, f32[512]{0:T(512)S(1)}, u32[]{:S(2)}, u32[]{:S(2)}) %collective-permute-start) | collective-permute-done | bytes 2080 | tf_op jit(solution)/shard_map/while/body/eval_jaxpr/ppermute | solution.py:14
  229.4 3.0 all-gather.5
  234.2 1.9 collective-permute-start
  236.2 4.2 %collective-permute-done = f32[512]{0:T(512)S(1)} collective-permute-done((f32[512]{0:T(512)S(1)}, f32[512]{0:T(512)S(1)}, u32[]{:S(2)}, u32[]{:S(2)}) %collective-permute-start) | collective-permute-done | bytes 2080 | tf_op jit(solution)/shard_map/while/body/eval_jaxpr/ppermute | solution.py:14
  240.4 3.0 all-gather.5
  245.2 1.9 collective-permute-start
  247.1 4.2 %collective-permute-done = f32[512]{0:T(512)S(1)} collective-permute-done((f32[512]{0:T(512)S(1)}, f32[512]{0:T(512)S(1)}, u32[]{:S(2)}, u32[]{:S(2)}) %collective-permute-start) | collective-permute-done | bytes 2080 | tf_op jit(solution)/shard_map/while/body/eval_jaxpr/ppermute | solution.py:14
  251.3 3.0 all-gather.5
  256.2 1.9 collective-permute-start
  258.1 4.2 %collective-permute-done = f32[512]{0:T(512)S(1)} collective-permute-done((f32[512]{0:T(512)S(1)}, f32[512]{0:T(512)S(1)}, u32[]{:S(2)}, u32[]{:S(2)}) %collective-permute-start) | collective-permute-done | bytes 2080 | tf_op jit(solution)/shard_map/while/body/eval_jaxpr/ppermute | solution.py:14
  262.3 3.0 all-gather.5
  267.2 1.9 collective-permute-start
  269.1 4.2 %collective-permute-done = f32[512]{0:T(512)S(1)} collective-permute-done((f32[512]{0:T(512)S(1)}, f32[512]{0:T(512)S(1)}, u32[]{:S(2)}, u32[]{:S(2)}) %collective-permute-start) | collective-permute-done | bytes 2080 | tf_op jit(solution)/shard_map/while/body/eval_jaxpr/ppermute | solution.py:14
  273.3 3.0 all-gather.5
  278.2 1.9 collective-permute-start
  280.1 4.2 %collective-permute-done = f32[512]{0:T(512)S(1)} collective-permute-done((f32[512]{0:T(512)S(1)}, f32[512]{0:T(512)S(1)}, u32[]{:S(2)}, u32[]{:S(2)}) %collective-permute-start) | collective-permute-done | bytes 2080 | tf_op jit(solution)/shard_map/while/body/eval_jaxpr/ppermute | solution.py:14
  284.3 3.0 all-gather.5
  289.1 1.9 collective-permute-start
  291.1 4.2 %collective-permute-done = f32[512]{0:T(512)S(1)} collective-permute-done((f32[512]{0:T(512)S(1)}, f32[512]{0:T(512)S(1)}, u32[]{:S(2)}, u32[]{:S(2)}) %collective-permute-start) | collective-permute-done | bytes 2080 | tf_op jit(solution)/shard_map/while/body/eval_jaxpr/ppermute | solution.py:14
  295.3 3.0 all-gather.5
  300.1 1.9 collective-permute-start
  302.1 4.2 %collective-permute-done = f32[512]{0:T(512)S(1)} collective-permute-done((f32[512]{0:T(512)S(1)}, f32[512]{0:T(512)S(1)}, u32[]{:S(2)}, u32[]{:S(2)}) %collective-permute-start) | collective-permute-done | bytes 2080 | tf_op jit(solution)/shard_map/while/body/eval_jaxpr/ppermute | solution.py:14
  306.3 3.0 all-gather.5
  311.1 1.9 collective-permute-start
  313.1 4.2 %collective-permute-done = f32[512]{0:T(512)S(1)} collective-permute-done((f32[512]{0:T(512)S(1)}, f32[512]{0:T(512)S(1)}, u32[]{:S(2)}, u32[]{:S(2)}) %collective-permute-start) | collective-permute-done | bytes 2080 | tf_op jit(solution)/shard_map/while/body/eval_jaxpr/ppermute | solution.py:14
  317.3 3.0 all-gather.5
  322.1 1.9 collective-permute-start
  324.0 4.2 %collective-permute-done = f32[512]{0:T(512)S(1)} collective-permute-done((f32[512]{0:T(512)S(1)}, f32[512]{0:T(512)S(1)}, u32[]{:S(2)}, u32[]{:S(2)}) %collective-permute-start) | collective-permute-done | bytes 2080 | tf_op jit(solution)/shard_map/while/body/eval_jaxpr/ppermute | solution.py:14
  328.2 3.0 all-gather.5
  333.1 1.9 collective-permute-start
  335.0 4.2 %collective-permute-done = f32[512]{0:T(512)S(1)} collective-permute-done((f32[512]{0:T(512)S(1)}, f32[512]{0:T(512)S(1)}, u32[]{:S(2)}, u32[]{:S(2)}) %collective-permute-start) | collective-permute-done | bytes 2080 | tf_op jit(solution)/shard_map/while/body/eval_jaxpr/ppermute | solution.py:14
  339.2 3.1 all-gather.2
  342.3 3.4 fusion.16
  347.6 1.9 fusion.17
  (93 shorter events, 42.6 us)
Async XLA Ops:
  6.5 10.6 %copy-start.5 = (s32[2048,1]{0,1:T(1,128)S(1)}, s32[2048,1]{0,1:T(1,128)}, u32[]{:S(2)}) copy-start(s32[2048,1]{0,1:T(1,128)} %param.11) | copy-start | bytes 24580
  6.5 101.5 %all-gather.9.cloned.1.call-start = ((), (), s32[]{:S(2)}) async-start(), calls=%async_computation.2 | async-start | bytes 6291456 | tf_op jit(solution)/shard_map/all_gather | solution.py:57
  93.6 72.3 %all-gather.11.cloned.1.call-start = ((), (), s32[]{:S(2)}) async-start(), calls=%async_computation.3 | async-start | bytes 6291456 | tf_op jit(solution)/shard_map/all_gather | solution.py:77
  93.7 14.4 %copy-start.3 = (bf16[2,16,64,512]{3,2,1,0:T(8,128)(2,1)S(1)}, bf16[2,16,64,512]{3,2,1,0:T(8,128)(2,1)}, u32[]{:S(2)}) copy-start(bf16[2,16,64,512]{3,2,1,0:T(8,128)(2,1)} %copy.18) | copy-start | bytes 6291460
  108.0 6.7 %copy-start = (f32[1024,1024]{1,0:T(8,128)S(1)}, f32[1024,1024]{1,0:T(8,128)}, u32[]{:S(2)}) copy-start(f32[1024,1024]{1,0:T(8,128)} %convert_add_fusion) | copy-start | bytes 12582916
  112.7 2.0 copy-start.4
  123.0 0.7 copy-start.6
  123.6 20.2 %copy-start.7 = (f32[1024]{0:T(1024)S(1)}, f32[1024]{0:T(1024)}, u32[]{:S(2)}) copy-start(f32[1024]{0:T(1024)} %param.7) | copy-start | bytes 12292
  137.4 11.5 %all-to-all-start.1 = ((bf16[2,16,64]{2,0,1:T(2,128)(2,1)}), bf16[2,16,64]{2,0,1:T(2,128)(2,1)S(1)}, u32[]{:S(2)}, u32[]{:S(2)}) async-start(bf16[2,16,64]{2,0,1:T(2,128)(2,1)} %copy.20), calls=%async_computation.1 | async-start | bytes 16384 | tf_op jit(solution)/shard_map/all_to_all | solution.py:50
  162.7 1.3 copy-start.1
  179.3 6.1 %collective-permute-start = (f32[512]{0:T(512)S(1)}, f32[512]{0:T(512)S(1)}, u32[]{:S(2)}, u32[]{:S(2)}) collective-permute-start(f32[512]{0:T(512)S(1)} %add.85), channel_id=1, source_target_pairs={{0,2},{2,4},{4,6},{6,8},{8,10},{10,12},{12,14},{14,16},{16,18},{18... | collective-permute-start | bytes 6152 | tf_op jit(solution)/shard_map/while/body/eval_jaxpr/ppermute | solution.py:14
  190.3 6.1 %collective-permute-start = (f32[512]{0:T(512)S(1)}, f32[512]{0:T(512)S(1)}, u32[]{:S(2)}, u32[]{:S(2)}) collective-permute-start(f32[512]{0:T(512)S(1)} %add.85), channel_id=1, source_target_pairs={{0,2},{2,4},{4,6},{6,8},{8,10},{10,12},{12,14},{14,16},{16,18},{18... | collective-permute-start | bytes 6152 | tf_op jit(solution)/shard_map/while/body/eval_jaxpr/ppermute | solution.py:14
  201.3 6.1 %collective-permute-start = (f32[512]{0:T(512)S(1)}, f32[512]{0:T(512)S(1)}, u32[]{:S(2)}, u32[]{:S(2)}) collective-permute-start(f32[512]{0:T(512)S(1)} %add.85), channel_id=1, source_target_pairs={{0,2},{2,4},{4,6},{6,8},{8,10},{10,12},{12,14},{14,16},{16,18},{18... | collective-permute-start | bytes 6152 | tf_op jit(solution)/shard_map/while/body/eval_jaxpr/ppermute | solution.py:14
  212.2 6.1 %collective-permute-start = (f32[512]{0:T(512)S(1)}, f32[512]{0:T(512)S(1)}, u32[]{:S(2)}, u32[]{:S(2)}) collective-permute-start(f32[512]{0:T(512)S(1)} %add.85), channel_id=1, source_target_pairs={{0,2},{2,4},{4,6},{6,8},{8,10},{10,12},{12,14},{14,16},{16,18},{18... | collective-permute-start | bytes 6152 | tf_op jit(solution)/shard_map/while/body/eval_jaxpr/ppermute | solution.py:14
  223.2 6.1 %collective-permute-start = (f32[512]{0:T(512)S(1)}, f32[512]{0:T(512)S(1)}, u32[]{:S(2)}, u32[]{:S(2)}) collective-permute-start(f32[512]{0:T(512)S(1)} %add.85), channel_id=1, source_target_pairs={{0,2},{2,4},{4,6},{6,8},{8,10},{10,12},{12,14},{14,16},{16,18},{18... | collective-permute-start | bytes 6152 | tf_op jit(solution)/shard_map/while/body/eval_jaxpr/ppermute | solution.py:14
  234.2 6.1 %collective-permute-start = (f32[512]{0:T(512)S(1)}, f32[512]{0:T(512)S(1)}, u32[]{:S(2)}, u32[]{:S(2)}) collective-permute-start(f32[512]{0:T(512)S(1)} %add.85), channel_id=1, source_target_pairs={{0,2},{2,4},{4,6},{6,8},{8,10},{10,12},{12,14},{14,16},{16,18},{18... | collective-permute-start | bytes 6152 | tf_op jit(solution)/shard_map/while/body/eval_jaxpr/ppermute | solution.py:14
  245.2 6.1 %collective-permute-start = (f32[512]{0:T(512)S(1)}, f32[512]{0:T(512)S(1)}, u32[]{:S(2)}, u32[]{:S(2)}) collective-permute-start(f32[512]{0:T(512)S(1)} %add.85), channel_id=1, source_target_pairs={{0,2},{2,4},{4,6},{6,8},{8,10},{10,12},{12,14},{14,16},{16,18},{18... | collective-permute-start | bytes 6152 | tf_op jit(solution)/shard_map/while/body/eval_jaxpr/ppermute | solution.py:14
  256.2 6.1 %collective-permute-start = (f32[512]{0:T(512)S(1)}, f32[512]{0:T(512)S(1)}, u32[]{:S(2)}, u32[]{:S(2)}) collective-permute-start(f32[512]{0:T(512)S(1)} %add.85), channel_id=1, source_target_pairs={{0,2},{2,4},{4,6},{6,8},{8,10},{10,12},{12,14},{14,16},{16,18},{18... | collective-permute-start | bytes 6152 | tf_op jit(solution)/shard_map/while/body/eval_jaxpr/ppermute | solution.py:14
  267.2 6.1 %collective-permute-start = (f32[512]{0:T(512)S(1)}, f32[512]{0:T(512)S(1)}, u32[]{:S(2)}, u32[]{:S(2)}) collective-permute-start(f32[512]{0:T(512)S(1)} %add.85), channel_id=1, source_target_pairs={{0,2},{2,4},{4,6},{6,8},{8,10},{10,12},{12,14},{14,16},{16,18},{18... | collective-permute-start | bytes 6152 | tf_op jit(solution)/shard_map/while/body/eval_jaxpr/ppermute | solution.py:14
  278.2 6.1 %collective-permute-start = (f32[512]{0:T(512)S(1)}, f32[512]{0:T(512)S(1)}, u32[]{:S(2)}, u32[]{:S(2)}) collective-permute-start(f32[512]{0:T(512)S(1)} %add.85), channel_id=1, source_target_pairs={{0,2},{2,4},{4,6},{6,8},{8,10},{10,12},{12,14},{14,16},{16,18},{18... | collective-permute-start | bytes 6152 | tf_op jit(solution)/shard_map/while/body/eval_jaxpr/ppermute | solution.py:14
  289.1 6.1 %collective-permute-start = (f32[512]{0:T(512)S(1)}, f32[512]{0:T(512)S(1)}, u32[]{:S(2)}, u32[]{:S(2)}) collective-permute-start(f32[512]{0:T(512)S(1)} %add.85), channel_id=1, source_target_pairs={{0,2},{2,4},{4,6},{6,8},{8,10},{10,12},{12,14},{14,16},{16,18},{18... | collective-permute-start | bytes 6152 | tf_op jit(solution)/shard_map/while/body/eval_jaxpr/ppermute | solution.py:14
  300.1 6.1 %collective-permute-start = (f32[512]{0:T(512)S(1)}, f32[512]{0:T(512)S(1)}, u32[]{:S(2)}, u32[]{:S(2)}) collective-permute-start(f32[512]{0:T(512)S(1)} %add.85), channel_id=1, source_target_pairs={{0,2},{2,4},{4,6},{6,8},{8,10},{10,12},{12,14},{14,16},{16,18},{18... | collective-permute-start | bytes 6152 | tf_op jit(solution)/shard_map/while/body/eval_jaxpr/ppermute | solution.py:14
  311.1 6.1 %collective-permute-start = (f32[512]{0:T(512)S(1)}, f32[512]{0:T(512)S(1)}, u32[]{:S(2)}, u32[]{:S(2)}) collective-permute-start(f32[512]{0:T(512)S(1)} %add.85), channel_id=1, source_target_pairs={{0,2},{2,4},{4,6},{6,8},{8,10},{10,12},{12,14},{14,16},{16,18},{18... | collective-permute-start | bytes 6152 | tf_op jit(solution)/shard_map/while/body/eval_jaxpr/ppermute | solution.py:14
  322.1 6.1 %collective-permute-start = (f32[512]{0:T(512)S(1)}, f32[512]{0:T(512)S(1)}, u32[]{:S(2)}, u32[]{:S(2)}) collective-permute-start(f32[512]{0:T(512)S(1)} %add.85), channel_id=1, source_target_pairs={{0,2},{2,4},{4,6},{6,8},{8,10},{10,12},{12,14},{14,16},{16,18},{18... | collective-permute-start | bytes 6152 | tf_op jit(solution)/shard_map/while/body/eval_jaxpr/ppermute | solution.py:14
  333.1 6.1 %collective-permute-start = (f32[512]{0:T(512)S(1)}, f32[512]{0:T(512)S(1)}, u32[]{:S(2)}, u32[]{:S(2)}) collective-permute-start(f32[512]{0:T(512)S(1)} %add.85), channel_id=1, source_target_pairs={{0,2},{2,4},{4,6},{6,8},{8,10},{10,12},{12,14},{14,16},{16,18},{18... | collective-permute-start | bytes 6152 | tf_op jit(solution)/shard_map/while/body/eval_jaxpr/ppermute | solution.py:14
  339.2 8.4 %copy-start.2 = (f32[512,1024]{1,0:T(8,128)S(1)}, f32[512,1024]{1,0:T(8,128)}, u32[]{:S(2)}) copy-start(f32[512,1024]{1,0:T(8,128)} %copy-done.1) | copy-start | bytes 6291460
Sparse Core Ops, SparseCore 0:
  93.7 14.2 all-gather.8
  123.1 14.8 all-gather.10
where the time goes:
time: 358 us; the launch traced here: 357 us
  blocking collectives  105 us (29%)
  waiting for transfers between devices  77.1 us (22%)
  matrix products  68.2 us (19%)
  local copies, waits for them, and re-layouts  40.7 us (11%)
  starting transfers between devices  35.6 us (10%)
  other arithmetic  16.2 us (5%)
  between operations  13.6 us (4%)
    ppermute x15, waiting for transfers between devices, shifted(): lax.ppermute(value, axis, [(source, source + steps) for source in range(f...  62.7 us
    all_to_all x1, blocking collectives, body(): lax.all_to_all(send_rows, 'tm', split_axis=1, concat_axis=1, tiled=True)  53.8 us
    all_gather x15, blocking collectives, advance(): whole_state = lax.all_gather(state_rows, 'row', axis=0, tiled=True)  43.5 us
    ppermute x15, starting transfers between devices, shifted(): lax.ppermute(value, axis, [(source, source + steps) for source in range(f...  29.1 us
    dot_general x15, matrix products, advance(): jnp.dot(composed, whole_state, precision=lax.Precision.HIGHEST)  28 us
    dot_general x2, matrix products, body(): jnp.dot(information[slab_index], evolve, precision=lax.Precision.HIGHEST)  18.4 us
    gather x1, local copies, waits for them, and re-layouts, body(): padded_values[slot_table].reshape(SLAB_DEV, time_devs, capacity)  13.1 us
    dot_general x1, matrix products, left_product(): new_matrix = jnp.dot(left_rows, pieces[0], precision=lax.Precision.HIGHEST)  9.65 us
  transfers between devices with their start and end apart: 18, of which 17 were waited for; matrix products, arithmetic and copies ran while one was open for 9% of the time, Pallas kernels for 0%

commit v1 on v0

--- a/solution.py
+++ b/solution.py
@@ -46,7 +46,12 @@
     send_rows = padded_rows[slot_table].reshape(SLAB_DEV, time_devs, capacity, local_cols)
     send_values = padded_values[slot_table].reshape(SLAB_DEV, time_devs, capacity)
     recv_rows, recv_values = (
-        lax.all_to_all(send_rows, "tm", split_axis=1, concat_axis=1, tiled=True),
+        jnp.concatenate(
+            lax.all_to_all(
+                jnp.stack(jnp.split(send_rows, lax.axis_size("tm"), axis=1)), "tm", 0, 0
+            ),
+            axis=1,
+        ),
         lax.all_to_all(send_values, "tm", split_axis=1, concat_axis=1, tiled=True),
     )
     slab_rows = recv_rows.reshape(SLAB_DEV, time_devs * capacity, local_cols)

time: 358 us -> 364 us (1.017)
  local copies, waits for them, and re-layouts: 40.7 us -> 46.5 us
    unnamed x17 -> x34, local copies, waits for them, and re-layouts: 3.97 us -> 11.6 us
where the time goes in v1:
time: 364 us; the launch traced here: 363 us
  blocking collectives  106 us (29%)
  waiting for transfers between devices  76.9 us (21%)
  matrix products  68.2 us (19%)
  local copies, waits for them, and re-layouts  46.5 us (13%)
  starting transfers between devices  35.8 us (10%)
  other arithmetic  16.2 us (4%)
  between operations  13.6 us (4%)
    ppermute x15, waiting for transfers between devices, shifted(): lax.ppermute(value, axis, [(source, source + steps) for source in range(f...  62.7 us
    all_to_all x1, blocking collectives, body(): lax.all_to_all(jnp.stack(jnp.split(send_rows, lax.axis_size('tm'), axis=1...  53.8 us
    all_gather x15, blocking collectives, advance(): whole_state = lax.all_gather(state_rows, 'row', axis=0, tiled=True)  43.5 us
    ppermute x15, starting transfers between devices, shifted(): lax.ppermute(value, axis, [(source, source + steps) for source in range(f...  29.1 us
    dot_general x15, matrix products, advance(): jnp.dot(composed, whole_state, precision=lax.Precision.HIGHEST)  28 us
    dot_general x2, matrix products, body(): jnp.dot(information[slab_index], evolve, precision=lax.Precision.HIGHEST)  18.4 us
    gather x1, local copies, waits for them, and re-layouts, body(): padded_values[slot_table].reshape(SLAB_DEV, time_devs, capacity)  13.1 us
    unnamed x34, local copies, waits for them, and re-layouts  11.6 us
  transfers between devices with their start and end apart: 18, of which 17 were waited for; matrix products, arithmetic and copies ran while one was open for 9% of the time, Pallas kernels for 0%

profile of v1, /device:TPU:9, one launch (start us, length us, event | category | flops | bytes accessed | tf_op | source)
XLA Modules:
  0.0 363.0 jit_solution(17604616806247130671)
XLA Ops:
  7.3 9.1 %reduce-window.6 = s32[32,16,128]{2,1,0:T(8,128)S(1)} reduce-window(s32[32,16,128]{2,1,0:T(8,128)S(1)} %fusion.4, s32[]{:T(128)} %copy.130), window={size=1x1x128 pad=0_0x0_0x127_0}, to_apply=%region_0.0 | reduce-window | flops 8323072 | bytes 524292 | tf_op jit(solution)/shard_map/reduce-window
  17.3 8.0 %scatter_custom_fusion = s32[2048]{0:T(1024)S(1)} fusion(s32[2048]{0:T(1024)S(1)} %bitcast.223, s32[2048]{0:T(1024)S(1)} %iota.23, s32[]{:T(128)} %constant.63.clone.1), kind=kCustom, calls=%fused_computation.66 | custom fusion | bytes 8196 | tf_op jit(solution)/shard_map/scatter | solution.py:42
  27.1 9.2 %gather_fusion = bf16[2048,512]{1,0:T(8,128)(2,1)} fusion(bf16[2049,512]{1,0:T(8,128)(2,1)S(1)} %concatenate.6, s32[2048]{0:T(1024)S(1)} %fusion.21), kind=kCustom, calls=%fused_computation | custom fusion | bytes 4202496 | tf_op jit(solution)/shard_map/gather | solution.py:46
  44.0 53.8 %all_to_all.10 = bf16[16,2,1,64,512]{4,3,1,2,0:T(8,128)(2,1)S(1)} all-to-all(bf16[16,2,1,64,512]{4,3,1,2,0:T(8,128)(2,1)S(1)} %fusion.5), channel_id=1, replica_groups=mesh['tm'=16,'row'=2] {'tm'}, dimensions={0} | all-to-all | bytes 4194304 | tf_op jit(solution)/shard_map/all_to_all | solution.py:50
  99.7 5.0 %convert_add_fusion = f32[1024,1024]{1,0:T(8,128)} fusion(f32[1024,1024]{1,0:T(8,128)} %param.8), kind=kLoop, calls=%fused_computation.4 | loop fusion | flops 3145728 | bytes 8388608 | tf_op jit(solution)/shard_map/add | solution.py:66
  104.7 9.2 %all-gather.9.cloned.1.call-done = bf16[2,1024,1024]{2,1,0:T(8,128)(2,1)} async-done(((bf16[2,1024,512]{2,1,0:T(8,128)(2,1)}), bf16[2,1024,1024]{2,1,0:T(8,128)(2,1)}) %all-gather.9.cloned.1.call-update) | async-done | bytes 4194320 | tf_op jit(solution)/shard_map/all_gather | solution.py:62
  113.9 4.7 %fusion.29 = f32[2,512,1024]{2,1,0:T(8,128)S(1)} fusion(bf16[2,1024,512]{2,1,0:T(8,128)(2,1)S(1)} %bitcast.183, bf16[2,1024,1024]{2,1,0:T(8,128)(2,1)} %all-gather.9.cloned.1.call-done), kind=kOutput, calls=%fused_computation.71 | convolution fusion | flops 2147483648 | bytes 10485760 | tf_op jit(solution)/shard_map/sra,srb->sab/dot_general | solution.py:59
  118.6 2.0 copy-done.5
  120.6 8.3 %multiply_subtract_fusion.1 = f32[512,1024]{1,0:T(8,128)} fusion(f32[1024,1024]{1,0:T(8,128)S(1)} %copy-done, s32[]{:T(128)S(6)} %select_n.38, f32[2,512,1024]{2,1,0:T(8,128)S(1)} %fusion.29), kind=kOutput, calls=%fused_computation.11 | convolution fusion | flops 6443499520 | bytes 10485764 | tf_op jit(solution)/shard_map/dot_general | solution.py:73
  129.5 13.1 %gather_fusion.1 = bf16[2048]{0:T(1024)(128)(2,1)S(1)} fusion(bf16[2049]{0:T(1024)(128)(2,1)S(1)} %pad_maximum_fusion, s32[2048]{0:T(1024)S(1)} %fusion.21), kind=kCustom, calls=%fused_computation.1 | custom fusion | bytes 16384 | tf_op jit(solution)/shard_map/gather | solution.py:47
  143.3 6.4 %all-to-all-start.1 = ((bf16[2,16,64]{2,0,1:T(2,128)(2,1)}), bf16[2,16,64]{2,0,1:T(2,128)(2,1)S(1)}, u32[]{:S(2)}, u32[]{:S(2)}) async-start(bf16[2,16,64]{2,0,1:T(2,128)(2,1)} %copy.82), calls=%async_computation.1 | async-start | bytes 16384 | tf_op jit(solution)/shard_map/all_to_all | solution.py:55
  149.8 5.0 %all-to-all-done.1 = bf16[2,16,64]{2,0,1:T(2,128)(2,1)S(1)} async-done(((bf16[2,16,64]{2,0,1:T(2,128)(2,1)}), bf16[2,16,64]{2,0,1:T(2,128)(2,1)S(1)}, u32[]{:S(2)}, u32[]{:S(2)}) %all-to-all-start.1) | async-done | bytes 4128 | tf_op jit(solution)/shard_map/all_to_all | solution.py:55
  155.3 3.4 all-gather
  158.6 10.1 %multiply_subtract_fusion = f32[512,1024]{1,0:T(8,128)S(1)} fusion(f32[1024,1024]{1,0:T(8,128)} %convert_add_fusion, s32[]{:T(128)S(6)} %select_n.38, f32[2,512,1024]{2,1,0:T(8,128)} %copy-done.5), kind=kOutput, calls=%fused_computation.10 | convolution fusion | flops 6443499520 | bytes 10485764 | tf_op jit(solution)/shard_map/dot_general | solution.py:73
  170.1 1.9 fusion.24
  172.0 9.7 %fusion.30 = f32[512,1024]{1,0:T(8,128)S(1)} fusion(f32[512,1024]{1,0:T(8,128)} %copy-done.1, f32[1024,1024]{1,0:T(8,128)} %all-gather.11.cloned.1.call-done), kind=kOutput, calls=%fused_computation.72 | convolution fusion | flops 6442450944 | bytes 8388608 | tf_op jit(solution)/shard_map/dot_general | solution.py:18
  181.6 163.7 %while.12 = (s32[]{:T(128)}, f32[512]{0:T(512)S(1)}, pred[]{:T(512)}, f32[512,1024]{1,0:T(8,128)S(1)}, f32[512]{0:T(512)S(1)}, /*index=5*/f32[512]{0:T(512)S(1)}, s32[]{:T(128)}) while((s32[]{:T(128)}, f32[512]{0:T(512)S(1)}, pred[]{:T(512)}, f32[512,1024]{1,0:T(8,128)S(1)}, f32[512]{0:T(512)S(1)}, /*index=5*/f32[512]{0:T(512)S(1)}, ...), condition=%wide.region_5.6_spmd, body=%wide.region_4.5_spmd.sunk | while | flops 6292482 | bytes 2130038 | solution.py:96
  185.4 2.2 collective-permute-start
  187.6 3.9 %collective-permute-done = f32[512]{0:T(512)S(1)} collective-permute-done((f32[512]{0:T(512)S(1)}, f32[512]{0:T(512)S(1)}, u32[]{:S(2)}, u32[]{:S(2)}) %collective-permute-start) | collective-permute-done | bytes 2080 | tf_op jit(solution)/shard_map/while/body/eval_jaxpr/ppermute | solution.py:14
  191.5 3.0 all-gather.5
  196.4 1.9 collective-permute-start
  198.3 4.2 %collective-permute-done = f32[512]{0:T(512)S(1)} collective-permute-done((f32[512]{0:T(512)S(1)}, f32[512]{0:T(512)S(1)}, u32[]{:S(2)}, u32[]{:S(2)}) %collective-permute-start) | collective-permute-done | bytes 2080 | tf_op jit(solution)/shard_map/while/body/eval_jaxpr/ppermute | solution.py:14
  202.5 3.0 all-gather.5
  207.3 1.9 collective-permute-start
  209.3 4.2 %collective-permute-done = f32[512]{0:T(512)S(1)} collective-permute-done((f32[512]{0:T(512)S(1)}, f32[512]{0:T(512)S(1)}, u32[]{:S(2)}, u32[]{:S(2)}) %collective-permute-start) | collective-permute-done | bytes 2080 | tf_op jit(solution)/shard_map/while/body/eval_jaxpr/ppermute | solution.py:14
  213.5 3.0 all-gather.5
  218.3 1.9 collective-permute-start
  220.3 4.2 %collective-permute-done = f32[512]{0:T(512)S(1)} collective-permute-done((f32[512]{0:T(512)S(1)}, f32[512]{0:T(512)S(1)}, u32[]{:S(2)}, u32[]{:S(2)}) %collective-permute-start) | collective-permute-done | bytes 2080 | tf_op jit(solution)/shard_map/while/body/eval_jaxpr/ppermute | solution.py:14
  224.5 3.0 all-gather.5
  229.3 1.9 collective-permute-start
  231.2 4.2 %collective-permute-done = f32[512]{0:T(512)S(1)} collective-permute-done((f32[512]{0:T(512)S(1)}, f32[512]{0:T(512)S(1)}, u32[]{:S(2)}, u32[]{:S(2)}) %collective-permute-start) | collective-permute-done | bytes 2080 | tf_op jit(solution)/shard_map/while/body/eval_jaxpr/ppermute | solution.py:14
  235.5 3.0 all-gather.5
  240.3 1.9 collective-permute-start
  242.2 4.2 %collective-permute-done = f32[512]{0:T(512)S(1)} collective-permute-done((f32[512]{0:T(512)S(1)}, f32[512]{0:T(512)S(1)}, u32[]{:S(2)}, u32[]{:S(2)}) %collective-permute-start) | collective-permute-done | bytes 2080 | tf_op jit(solution)/shard_map/while/body/eval_jaxpr/ppermute | solution.py:14
  246.4 3.0 all-gather.5
  251.3 1.9 collective-permute-start
  253.2 4.2 %collective-permute-done = f32[512]{0:T(512)S(1)} collective-permute-done((f32[512]{0:T(512)S(1)}, f32[512]{0:T(512)S(1)}, u32[]{:S(2)}, u32[]{:S(2)}) %collective-permute-start) | collective-permute-done | bytes 2080 | tf_op jit(solution)/shard_map/while/body/eval_jaxpr/ppermute | solution.py:14
  257.4 3.0 all-gather.5
  262.3 1.9 collective-permute-start
  264.2 4.2 %collective-permute-done = f32[512]{0:T(512)S(1)} collective-permute-done((f32[512]{0:T(512)S(1)}, f32[512]{0:T(512)S(1)}, u32[]{:S(2)}, u32[]{:S(2)}) %collective-permute-start) | collective-permute-done | bytes 2080 | tf_op jit(solution)/shard_map/while/body/eval_jaxpr/ppermute | solution.py:14
  268.4 3.0 all-gather.5
  273.3 1.9 collective-permute-start
  275.2 4.2 %collective-permute-done = f32[512]{0:T(512)S(1)} collective-permute-done((f32[512]{0:T(512)S(1)}, f32[512]{0:T(512)S(1)}, u32[]{:S(2)}, u32[]{:S(2)}) %collective-permute-start) | collective-permute-done | bytes 2080 | tf_op jit(solution)/shard_map/while/body/eval_jaxpr/ppermute | solution.py:14
  279.4 3.0 all-gather.5
  284.2 1.9 collective-permute-start
  286.2 4.2 %collective-permute-done = f32[512]{0:T(512)S(1)} collective-permute-done((f32[512]{0:T(512)S(1)}, f32[512]{0:T(512)S(1)}, u32[]{:S(2)}, u32[]{:S(2)}) %collective-permute-start) | collective-permute-done | bytes 2080 | tf_op jit(solution)/shard_map/while/body/eval_jaxpr/ppermute | solution.py:14
  290.4 3.0 all-gather.5
  295.2 1.9 collective-permute-start
  297.2 4.2 %collective-permute-done = f32[512]{0:T(512)S(1)} collective-permute-done((f32[512]{0:T(512)S(1)}, f32[512]{0:T(512)S(1)}, u32[]{:S(2)}, u32[]{:S(2)}) %collective-permute-start) | collective-permute-done | bytes 2080 | tf_op jit(solution)/shard_map/while/body/eval_jaxpr/ppermute | solution.py:14
  301.4 3.0 all-gather.5
  306.2 1.9 collective-permute-start
  308.2 4.2 %collective-permute-done = f32[512]{0:T(512)S(1)} collective-permute-done((f32[512]{0:T(512)S(1)}, f32[512]{0:T(512)S(1)}, u32[]{:S(2)}, u32[]{:S(2)}) %collective-permute-start) | collective-permute-done | bytes 2080 | tf_op jit(solution)/shard_map/while/body/eval_jaxpr/ppermute | solution.py:14
  312.4 3.0 all-gather.5
  317.2 1.9 collective-permute-start
  319.1 4.2 %collective-permute-done = f32[512]{0:T(512)S(1)} collective-permute-done((f32[512]{0:T(512)S(1)}, f32[512]{0:T(512)S(1)}, u32[]{:S(2)}, u32[]{:S(2)}) %collective-permute-start) | collective-permute-done | bytes 2080 | tf_op jit(solution)/shard_map/while/body/eval_jaxpr/ppermute | solution.py:14
  323.3 3.0 all-gather.5
  328.2 1.9 collective-permute-start
  330.1 4.2 %collective-permute-done = f32[512]{0:T(512)S(1)} collective-permute-done((f32[512]{0:T(512)S(1)}, f32[512]{0:T(512)S(1)}, u32[]{:S(2)}, u32[]{:S(2)}) %collective-permute-start) | collective-permute-done | bytes 2080 | tf_op jit(solution)/shard_map/while/body/eval_jaxpr/ppermute | solution.py:14
  334.3 3.0 all-gather.5
  339.2 1.9 collective-permute-start
  341.1 4.2 %collective-permute-done = f32[512]{0:T(512)S(1)} collective-permute-done((f32[512]{0:T(512)S(1)}, f32[512]{0:T(512)S(1)}, u32[]{:S(2)}, u32[]{:S(2)}) %collective-permute-start) | collective-permute-done | bytes 2080 | tf_op jit(solution)/shard_map/while/body/eval_jaxpr/ppermute | solution.py:14
  345.3 3.1 all-gather.2
  348.4 3.4 fusion.32
  353.7 1.9 fusion.33
  (110 shorter events, 48.6 us)
Async XLA Ops:
  6.5 10.6 %copy-start.6 = (s32[2048,1]{0,1:T(1,128)S(1)}, s32[2048,1]{0,1:T(1,128)}, u32[]{:S(2)}) copy-start(s32[2048,1]{0,1:T(1,128)} %param.11) | copy-start | bytes 24580
  6.5 107.3 %all-gather.9.cloned.1.call-start = ((), (), s32[]{:S(2)}) async-start(), calls=%async_computation.2 | async-start | bytes 6291456 | tf_op jit(solution)/shard_map/all_gather | solution.py:62
  36.3 7.5 %copy-start.4 = (bf16[2048,512]{1,0:T(8,128)(2,1)S(1)}, bf16[2048,512]{1,0:T(8,128)(2,1)}, u32[]{:S(2)}) copy-start(bf16[2048,512]{1,0:T(8,128)(2,1)} %gather_fusion) | copy-start | bytes 6291460
  99.5 72.5 %all-gather.11.cloned.1.call-start = ((), (), s32[]{:S(2)}) async-start(), calls=%async_computation.3 | async-start | bytes 6291456 | tf_op jit(solution)/shard_map/all_gather | solution.py:82
  99.7 14.2 %copy-start.3 = (bf16[2,16,1,64,512]{4,3,1,0,2:T(8,128)(2,1)S(1)}, bf16[2,16,1,64,512]{4,3,1,0,2:T(8,128)(2,1)}, u32[]{:S(2)}) copy-start(bf16[2,16,1,64,512]{4,3,1,0,2:T(8,128)(2,1)} %copy.80) | copy-start | bytes 6291460
  113.9 6.7 %copy-start = (f32[1024,1024]{1,0:T(8,128)S(1)}, f32[1024,1024]{1,0:T(8,128)}, u32[]{:S(2)}) copy-start(f32[1024,1024]{1,0:T(8,128)} %convert_add_fusion) | copy-start | bytes 12582916
  118.6 2.0 copy-start.5
  128.8 0.7 copy-start.7
  129.5 20.2 %copy-start.8 = (f32[1024]{0:T(1024)S(1)}, f32[1024]{0:T(1024)}, u32[]{:S(2)}) copy-start(f32[1024]{0:T(1024)} %param.7) | copy-start | bytes 12292
  143.3 11.5 %all-to-all-start.1 = ((bf16[2,16,64]{2,0,1:T(2,128)(2,1)}), bf16[2,16,64]{2,0,1:T(2,128)(2,1)S(1)}, u32[]{:S(2)}, u32[]{:S(2)}) async-start(bf16[2,16,64]{2,0,1:T(2,128)(2,1)} %copy.82), calls=%async_computation.1 | async-start | bytes 16384 | tf_op jit(solution)/shard_map/all_to_all | solution.py:55
  168.8 1.3 copy-start.1
  185.4 6.1 %collective-permute-start = (f32[512]{0:T(512)S(1)}, f32[512]{0:T(512)S(1)}, u32[]{:S(2)}, u32[]{:S(2)}) collective-permute-start(f32[512]{0:T(512)S(1)} %add.85), channel_id=1, source_target_pairs={{0,2},{2,4},{4,6},{6,8},{8,10},{10,12},{12,14},{14,16},{16,18},{18... | collective-permute-start | bytes 6152 | tf_op jit(solution)/shard_map/while/body/eval_jaxpr/ppermute | solution.py:14
  196.4 6.1 %collective-permute-start = (f32[512]{0:T(512)S(1)}, f32[512]{0:T(512)S(1)}, u32[]{:S(2)}, u32[]{:S(2)}) collective-permute-start(f32[512]{0:T(512)S(1)} %add.85), channel_id=1, source_target_pairs={{0,2},{2,4},{4,6},{6,8},{8,10},{10,12},{12,14},{14,16},{16,18},{18... | collective-permute-start | bytes 6152 | tf_op jit(solution)/shard_map/while/body/eval_jaxpr/ppermute | solution.py:14
  207.3 6.1 %collective-permute-start = (f32[512]{0:T(512)S(1)}, f32[512]{0:T(512)S(1)}, u32[]{:S(2)}, u32[]{:S(2)}) collective-permute-start(f32[512]{0:T(512)S(1)} %add.85), channel_id=1, source_target_pairs={{0,2},{2,4},{4,6},{6,8},{8,10},{10,12},{12,14},{14,16},{16,18},{18... | collective-permute-start | bytes 6152 | tf_op jit(solution)/shard_map/while/body/eval_jaxpr/ppermute | solution.py:14
  218.3 6.1 %collective-permute-start = (f32[512]{0:T(512)S(1)}, f32[512]{0:T(512)S(1)}, u32[]{:S(2)}, u32[]{:S(2)}) collective-permute-start(f32[512]{0:T(512)S(1)} %add.85), channel_id=1, source_target_pairs={{0,2},{2,4},{4,6},{6,8},{8,10},{10,12},{12,14},{14,16},{16,18},{18... | collective-permute-start | bytes 6152 | tf_op jit(solution)/shard_map/while/body/eval_jaxpr/ppermute | solution.py:14
  229.3 6.1 %collective-permute-start = (f32[512]{0:T(512)S(1)}, f32[512]{0:T(512)S(1)}, u32[]{:S(2)}, u32[]{:S(2)}) collective-permute-start(f32[512]{0:T(512)S(1)} %add.85), channel_id=1, source_target_pairs={{0,2},{2,4},{4,6},{6,8},{8,10},{10,12},{12,14},{14,16},{16,18},{18... | collective-permute-start | bytes 6152 | tf_op jit(solution)/shard_map/while/body/eval_jaxpr/ppermute | solution.py:14
  240.3 6.1 %collective-permute-start = (f32[512]{0:T(512)S(1)}, f32[512]{0:T(512)S(1)}, u32[]{:S(2)}, u32[]{:S(2)}) collective-permute-start(f32[512]{0:T(512)S(1)} %add.85), channel_id=1, source_target_pairs={{0,2},{2,4},{4,6},{6,8},{8,10},{10,12},{12,14},{14,16},{16,18},{18... | collective-permute-start | bytes 6152 | tf_op jit(solution)/shard_map/while/body/eval_jaxpr/ppermute | solution.py:14
  251.3 6.1 %collective-permute-start = (f32[512]{0:T(512)S(1)}, f32[512]{0:T(512)S(1)}, u32[]{:S(2)}, u32[]{:S(2)}) collective-permute-start(f32[512]{0:T(512)S(1)} %add.85), channel_id=1, source_target_pairs={{0,2},{2,4},{4,6},{6,8},{8,10},{10,12},{12,14},{14,16},{16,18},{18... | collective-permute-start | bytes 6152 | tf_op jit(solution)/shard_map/while/body/eval_jaxpr/ppermute | solution.py:14
  262.3 6.1 %collective-permute-start = (f32[512]{0:T(512)S(1)}, f32[512]{0:T(512)S(1)}, u32[]{:S(2)}, u32[]{:S(2)}) collective-permute-start(f32[512]{0:T(512)S(1)} %add.85), channel_id=1, source_target_pairs={{0,2},{2,4},{4,6},{6,8},{8,10},{10,12},{12,14},{14,16},{16,18},{18... | collective-permute-start | bytes 6152 | tf_op jit(solution)/shard_map/while/body/eval_jaxpr/ppermute | solution.py:14
  273.3 6.1 %collective-permute-start = (f32[512]{0:T(512)S(1)}, f32[512]{0:T(512)S(1)}, u32[]{:S(2)}, u32[]{:S(2)}) collective-permute-start(f32[512]{0:T(512)S(1)} %add.85), channel_id=1, source_target_pairs={{0,2},{2,4},{4,6},{6,8},{8,10},{10,12},{12,14},{14,16},{16,18},{18... | collective-permute-start | bytes 6152 | tf_op jit(solution)/shard_map/while/body/eval_jaxpr/ppermute | solution.py:14
  284.2 6.1 %collective-permute-start = (f32[512]{0:T(512)S(1)}, f32[512]{0:T(512)S(1)}, u32[]{:S(2)}, u32[]{:S(2)}) collective-permute-start(f32[512]{0:T(512)S(1)} %add.85), channel_id=1, source_target_pairs={{0,2},{2,4},{4,6},{6,8},{8,10},{10,12},{12,14},{14,16},{16,18},{18... | collective-permute-start | bytes 6152 | tf_op jit(solution)/shard_map/while/body/eval_jaxpr/ppermute | solution.py:14
  295.2 6.1 %collective-permute-start = (f32[512]{0:T(512)S(1)}, f32[512]{0:T(512)S(1)}, u32[]{:S(2)}, u32[]{:S(2)}) collective-permute-start(f32[512]{0:T(512)S(1)} %add.85), channel_id=1, source_target_pairs={{0,2},{2,4},{4,6},{6,8},{8,10},{10,12},{12,14},{14,16},{16,18},{18... | collective-permute-start | bytes 6152 | tf_op jit(solution)/shard_map/while/body/eval_jaxpr/ppermute | solution.py:14
  306.2 6.1 %collective-permute-start = (f32[512]{0:T(512)S(1)}, f32[512]{0:T(512)S(1)}, u32[]{:S(2)}, u32[]{:S(2)}) collective-permute-start(f32[512]{0:T(512)S(1)} %add.85), channel_id=1, source_target_pairs={{0,2},{2,4},{4,6},{6,8},{8,10},{10,12},{12,14},{14,16},{16,18},{18... | collective-permute-start | bytes 6152 | tf_op jit(solution)/shard_map/while/body/eval_jaxpr/ppermute | solution.py:14
  317.2 6.1 %collective-permute-start = (f32[512]{0:T(512)S(1)}, f32[512]{0:T(512)S(1)}, u32[]{:S(2)}, u32[]{:S(2)}) collective-permute-start(f32[512]{0:T(512)S(1)} %add.85), channel_id=1, source_target_pairs={{0,2},{2,4},{4,6},{6,8},{8,10},{10,12},{12,14},{14,16},{16,18},{18... | collective-permute-start | bytes 6152 | tf_op jit(solution)/shard_map/while/body/eval_jaxpr/ppermute | solution.py:14
  328.2 6.1 %collective-permute-start = (f32[512]{0:T(512)S(1)}, f32[512]{0:T(512)S(1)}, u32[]{:S(2)}, u32[]{:S(2)}) collective-permute-start(f32[512]{0:T(512)S(1)} %add.85), channel_id=1, source_target_pairs={{0,2},{2,4},{4,6},{6,8},{8,10},{10,12},{12,14},{14,16},{16,18},{18... | collective-permute-start | bytes 6152 | tf_op jit(solution)/shard_map/while/body/eval_jaxpr/ppermute | solution.py:14
  339.2 6.1 %collective-permute-start = (f32[512]{0:T(512)S(1)}, f32[512]{0:T(512)S(1)}, u32[]{:S(2)}, u32[]{:S(2)}) collective-permute-start(f32[512]{0:T(512)S(1)} %add.85), channel_id=1, source_target_pairs={{0,2},{2,4},{4,6},{6,8},{8,10},{10,12},{12,14},{14,16},{16,18},{18... | collective-permute-start | bytes 6152 | tf_op jit(solution)/shard_map/while/body/eval_jaxpr/ppermute | solution.py:14
  345.3 8.4 %copy-start.2 = (f32[512,1024]{1,0:T(8,128)S(1)}, f32[512,1024]{1,0:T(8,128)}, u32[]{:S(2)}) copy-start(f32[512,1024]{1,0:T(8,128)} %copy-done.1) | copy-start | bytes 6291460
Sparse Core Ops, SparseCore 0:
  99.6 14.2 all-gather.8
  129.0 14.8 all-gather.10
